TPU v7x, 128 devices: a whole 4x4x4 slice. The times are simulated.
128 devices in a mesh: region: 16 (over y_lo, z, core), group: 8 (over y_hi, x).
Axes of the slice: x: 4, y: 4 (y_hi: 2, y_lo: 2; y = y_hi * 2 + y_lo), z: 4, core: 2. Of those that a mesh axis runs over, the one named last changes fastest.
Arguments:
- object_slab: float32 [8192, 2, 4096], P('region', None, 'group'), may hold values from -6 to 6
- probe: float32 [4, 2, 256, 256], replicated, may hold values from -6 to 6
- diffraction: float32 [512, 256, 256], P(('region', 'group')), may hold values from 0.25 to 16
- positions: int32 [512, 2], P(('region', 'group')), may hold values from 0 to 7936, as said below
- slot_counts: int32 [8, 16], P('group', 'region'), may hold values from 1 to 4, 40 in all within a row
Outputs:
- new_object: float32 [8192, 2, 4096], P('region', None, 'group')
- new_probe: float32 [4, 2, 256, 256], replicated
Inputs may be any that keep to these rules, and one draw needn't show every extreme that they name: `positions`: A slot of region index r has its row in r * 512 to min(r * 512 + 511, 7936); columns lie in 0 to 256; rows 0 and 7936 and columns 0 and 256 are each taken by some slot.
All inputs are finite; a program needn't handle non-finite values. No bound on the sum of `slot_counts` on one device may be relied on, other than what follows from the above.
Results may differ from a plain program's by a relative error of at most 0.0003.
Values sent between devices are 32-bit elements; how exact they have to be, the bound alone decides.
A program may use at most 128 MiB of HBM per device.

v0:
```python
import math
import jax
import jax.numpy as jnp
from jax import lax
from jax.sharding import PartitionSpec as P

highest = lax.Precision.HIGHEST


def shifted(block, axis, distance):
    devices = range(lax.axis_size(axis))
    route = [(i - distance, i) for i in devices if i - distance in devices]
    return lax.ppermute(block, axis, route)


def tables(side):
    index = jnp.arange(side, dtype=jnp.int32)
    prod = index[:, None] * index[None, :] % side
    angle = prod.astype(jnp.float32) * (2.0 * math.pi / side)
    scale = 1.0 / math.sqrt(side)
    return (jnp.cos(angle) * scale, -jnp.sin(angle) * scale)


def transform(real_part, imag_part, cos_tab, sin_tab):
    left_r = jnp.einsum("jk,mkl->mjl", cos_tab, real_part, precision=highest) - jnp.einsum(
        "jk,mkl->mjl", sin_tab, imag_part, precision=highest
    )
    left_i = jnp.einsum("jk,mkl->mjl", cos_tab, imag_part, precision=highest) + jnp.einsum(
        "jk,mkl->mjl", sin_tab, real_part, precision=highest
    )
    out_r = jnp.einsum("mjk,kl->mjl", left_r, cos_tab, precision=highest) - jnp.einsum(
        "mjk,kl->mjl", left_i, sin_tab, precision=highest
    )
    out_i = jnp.einsum("mjk,kl->mjl", left_r, sin_tab, precision=highest) + jnp.einsum(
        "mjk,kl->mjl", left_i, cos_tab, precision=highest
    )
    return (out_r, out_i)


def on_device(object_slab, probe, diffraction, positions, slot_counts):
    side = probe.shape[2]
    slots = diffraction.shape[0]
    tile_rows = object_slab.shape[0]
    active_count = slot_counts[0, 0]
    cos_tab, sin_tab = tables(side)
    base = lax.axis_index("region") * tile_rows
    local_rows = positions[:, 0] - base
    shard_columns = positions[:, 1]
    obj = object_slab
    prb = probe
    peak = jnp.max(jnp.sum(prb[:, 0] * prb[:, 0] + prb[:, 1] * prb[:, 1], axis=0))
    below = shifted(obj, "region", -1)
    extended = jnp.concatenate([obj, below], axis=0)

    def cut(row, col):
        return lax.dynamic_slice(extended, (row, jnp.int32(0), col), (side, 2, side))

    windows = jax.vmap(cut)(local_rows, shard_columns)
    probe_r = prb[:, 0]
    probe_i = prb[:, 1]

    def single_position(position_entry, carry):
        wgrads, pgrad, cover = carry
        live = (position_entry < active_count).astype(jnp.float32)
        win = lax.dynamic_index_in_dim(windows, position_entry, 0, keepdims=False)
        observed_intensity = lax.dynamic_index_in_dim(
            diffraction, position_entry, 0, keepdims=False
        )
        win_r = win[:, 0, :]
        win_i = win[:, 1, :]
        exit_r = probe_r * win_r[None] - probe_i * win_i[None]
        exit_i = probe_r * win_i[None] + probe_i * win_r[None]
        far_r, far_i = transform(exit_r, exit_i, cos_tab, sin_tab)
        model_intensity = jnp.sum(far_r * far_r + far_i * far_i, axis=0)
        update_ratio = 1.0 - jnp.sqrt(observed_intensity) / jnp.sqrt(
            jnp.maximum(model_intensity, 1.0)
        )
        chi_r, chi_i = transform(
            far_r * update_ratio[None], far_i * update_ratio[None], cos_tab, -sin_tab
        )
        chi_r = chi_r * live
        chi_i = chi_i * live
        go_r = jnp.sum(probe_r * chi_r + probe_i * chi_i, axis=0)
        go_i = jnp.sum(probe_r * chi_i - probe_i * chi_r, axis=0)
        grad_win = jnp.stack([go_r, go_i], axis=1)
        wgrads = lax.dynamic_update_index_in_dim(wgrads, grad_win, position_entry, 0)
        gp = jnp.stack(
            [win_r[None] * chi_r + win_i[None] * chi_i, win_r[None] * chi_i - win_i[None] * chi_r],
            axis=1,
        )
        return (wgrads, pgrad + gp, cover + live * (win_r * win_r + win_i * win_i))

    start_carry = (
        jnp.zeros((slots, side, 2, side), jnp.float32),
        jnp.zeros(prb.shape, jnp.float32),
        jnp.zeros((side, side), jnp.float32),
    )
    wgrads, pgrad, cover = lax.fori_loop(0, slots, single_position, start_carry)
    pgrad, cover = lax.psum((pgrad, cover), ("region", "group"))

    def put(position_entry, scratch_array):
        row = local_rows[position_entry]
        col = shard_columns[position_entry]
        current = lax.dynamic_slice(scratch_array, (row, jnp.int32(0), col), (side, 2, side))
        return lax.dynamic_update_slice(
            scratch_array, current + wgrads[position_entry], (row, jnp.int32(0), col)
        )

    scratch_array = lax.fori_loop(0, slots, put, jnp.zeros(extended.shape, jnp.float32))
    tile_grad = scratch_array[:tile_rows]
    spill = scratch_array[tile_rows:]
    arrived = shifted(spill, "region", 1)
    tile_grad = tile_grad + arrived
    obj = obj - tile_grad / peak
    prb = prb - pgrad / (cover + 1e-06)[None, None]
    return (obj, prb)


def solution(mesh):
    placed = (
        P("region", None, "group"),
        P(),
        P(("region", "group"), None, None),
        P(("region", "group"), None),
        P("group", "region"),
    )
    return jax.shard_map(
        on_device,
        mesh=mesh,
        in_specs=placed,
        out_specs=(P("region", None, "group"), P()),
        check_vma=False,
    )
```

profile of v0, /device:TPU:1, one launch (start us, length us, event | category | flops | bytes accessed | tf_op | source)
XLA Modules:
  0.0 704.6 jit_solution(1375702932699397892)
XLA Ops:
  13.6 22.5 %collective-permute-done = f32[512,2,512]{2,1,0:T(2,128)} collective-permute-done((f32[512,2,512]{2,1,0:T(2,128)}, f32[512,2,512]{2,1,0:T(2,128)}, u32[]{:S(2)}, u32[]{:S(2)}) %collective-permute-start) | collective-permute-done | bytes 2097184 | tf_op jit(solution)/shard_map/ppermute | solution.py:13
  36.2 5.3 pad_maximum_fusion
  43.4 17.1 %while.35 = (s32[]{:T(128)}, f32[1024,2,512]{2,1,0:T(2,128)}, s32[4,3]{1,0:T(4,128)S(1)}, f32[4,256,2,256]{3,2,1,0:T(2,128)}, s32[]{:T(128)}) while((s32[]{:T(128)}, f32[1024,2,512]{2,1,0:T(2,128)}, s32[4,3]{1,0:T(4,128)S(1)}, f32[4,256,2,256]{3,2,1,0:T(2,128)}, s32[]{:T(128)}) %tuple.99), condition=%wide.while_cond, body=%wide.while_body.sunk | while | flops 2 | bytes 1050217 | solution.py:56
  43.9 3.7 bitcast_dynamic-update-slice_fusion.2
  48.2 3.7 bitcast_dynamic-update-slice_fusion.2
  52.5 3.7 bitcast_dynamic-update-slice_fusion.2
  56.8 3.7 bitcast_dynamic-update-slice_fusion.2
  62.3 249.9 %while.36 = (s32[]{:T(128)}, f32[4,256,2,256]{3,2,1,0:T(2,128)}, f32[4,2,256,256]{3,2,0,1:T(8,128)}, f32[256,256]{1,0:T(8,128)}, f32[4,256,2,256]{3,2,1,0:T(2,12...) while((s32[]{:T(128)}, f32[4,256,2,256]{3,2,1,0:T(2,128)}, ...), condition=%wide.region_4.5_spmd.clone.clone, body=%wide.region_0.4_spmd.clone.clone.sunk | while | flops 12915048448 | bytes 82838280 | solution.py:98
  100.1 3.7 fusion.229
  104.4 4.6 fusion.232
  111.7 5.4 add_bitcast_fusion.2
  160.1 3.7 fusion.229
  164.5 4.8 fusion.232
  172.0 5.4 add_bitcast_fusion.2
  177.3 3.9 maximum_add_fusion.2
  212.0 3.7 fusion.231
  222.1 3.7 fusion.229
  226.4 4.5 fusion.232
  233.6 5.4 add_bitcast_fusion.2
  239.0 3.9 maximum_add_fusion.2
  283.7 3.7 fusion.229
  288.1 4.6 fusion.232
  295.3 5.4 add_bitcast_fusion.2
  300.7 3.9 maximum_add_fusion.2
  315.3 207.1 %while.34 = (s32[]{:T(128)}, f32[1024,2,512]{2,1,0:T(2,128)}, s32[4]{0:T(128)S(1)}, s32[4]{0:T(128)S(1)}, f32[4,256,2,256]{3,2,1,0:T(2,128)}, /*index=5*/s32[]{:T(128)}, s32[]{:T(128)}, s32[]{:T(128)}, s32[]{:T(128)}) while((s32[]{:T(128)}, f32[1024,2,512]{2,1,0:T(2,128)}, s32[4]{0:T(128)S(1)}, s32[4]{0:T(128)S(1)}, ...), condition=%wide.region_6.7_spmd, body=%wide.region_5.6_spmd.sunk | while | flops 131080 | bytes 2621641 | solution.py:109
  322.1 45.0 %dynamic_update_slice.21 = f32[1024,2,512]{2,1,0:T(2,128)} dynamic-update-slice(f32[1024,2,512]{2,1,0:T(2,128)} %get-tuple-element.735, f32[256,2,256]{2,1,0:T(2,128)S(1)} %bitcast_add_fusion.2, s32[]{:T(128)S(6)} %select_n.175, s32[]{:T(128)} %constant.116.clone.1..sunk, s32[]{:T(128)S(6)} %select_n.176) | dynamic-update-slice | bytes 1048580 | tf_op jit(solution)/shard_map/while/body/eval_jaxpr/dynamic_update_slice | solution.py:105
  373.8 45.0 %dynamic_update_slice.21 = f32[1024,2,512]{2,1,0:T(2,128)} dynamic-update-slice(f32[1024,2,512]{2,1,0:T(2,128)} %get-tuple-element.735, f32[256,2,256]{2,1,0:T(2,128)S(1)} %bitcast_add_fusion.2, s32[]{:T(128)S(6)} %select_n.175, s32[]{:T(128)} %constant.116.clone.1..sunk, s32[]{:T(128)S(6)} %select_n.176) | dynamic-update-slice | bytes 1048580 | tf_op jit(solution)/shard_map/while/body/eval_jaxpr/dynamic_update_slice | solution.py:105
  425.6 45.0 %dynamic_update_slice.21 = f32[1024,2,512]{2,1,0:T(2,128)} dynamic-update-slice(f32[1024,2,512]{2,1,0:T(2,128)} %get-tuple-element.735, f32[256,2,256]{2,1,0:T(2,128)S(1)} %bitcast_add_fusion.2, s32[]{:T(128)S(6)} %select_n.175, s32[]{:T(128)} %constant.116.clone.1..sunk, s32[]{:T(128)S(6)} %select_n.176) | dynamic-update-slice | bytes 1048580 | tf_op jit(solution)/shard_map/while/body/eval_jaxpr/dynamic_update_slice | solution.py:105
  477.4 45.0 %dynamic_update_slice.21 = f32[1024,2,512]{2,1,0:T(2,128)} dynamic-update-slice(f32[1024,2,512]{2,1,0:T(2,128)} %get-tuple-element.735, f32[256,2,256]{2,1,0:T(2,128)S(1)} %bitcast_add_fusion.2, s32[]{:T(128)S(6)} %select_n.175, s32[]{:T(128)} %constant.116.clone.1..sunk, s32[]{:T(128)S(6)} %select_n.176) | dynamic-update-slice | bytes 1048580 | tf_op jit(solution)/shard_map/while/body/eval_jaxpr/dynamic_update_slice | solution.py:105
  522.3 3.8 slice.43
  532.0 155.4 %all-reduce.3.cloned.1.call-done = (f32[4,2,256,256]{3,2,1,0:T(8,128)}, f32[256,256]{1,0:T(8,128)}) async-done(((f32[4,2,256,256]{3,2,1,0:T(8,128)}, f32[256,256]{1,0:T(8,128)}), (f32[4,2,256,256]{3,2,1,0:T(8,128)}, f32[256,256]{1,0:T(8,128)})) %all-reduce.3.cloned.1.call-update) | async-done | bytes 2359312 | tf_op jit(solution)/shard_map/psum | solution.py:99
  692.7 4.9 divide_subtract_fusion
  (169 shorter events, 210.5 us)
Async XLA Ops:
  7.2 680.3 %all-reduce.3.cloned.1.call-start = ((), (), s32[]{:S(2)}) async-start(), calls=%async_computation | async-start | bytes 4718592 | tf_op jit(solution)/shard_map/psum | solution.py:99
  7.2 29.0 %collective-permute-start = (f32[512,2,512]{2,1,0:T(2,128)}, f32[512,2,512]{2,1,0:T(2,128)}, u32[]{:S(2)}, u32[]{:S(2)}) collective-permute-start(f32[512,2,512]{2,1,0:T(2,128)} %param.9), channel_id=1, source_target_pairs={{8,0},{16,8},{24,16},{32,24},{40,32},{48,40},{56,48},{64,56},{72,6... | collective-permute-start | bytes 6291464 | tf_op jit(solution)/shard_map/ppermute | solution.py:13
  11.7 24.5 %copy-start.7 = (f32[512,2,512]{2,1,0:T(2,128)S(1)}, f32[512,2,512]{2,1,0:T(2,128)}, u32[]{:S(2)}) copy-start(f32[512,2,512]{2,1,0:T(2,128)} %param.9) | copy-start | bytes 6291460
  99.0 1.0 copy-start.1
  104.4 4.6 copy-start.2
  104.4 7.3 %copy-start = (f32[4,256,256]{1,2,0:T(8,128)S(1)}, f32[4,256,256]{1,2,0:T(8,128)}, u32[]{:S(2)}) copy-start(f32[4,256,256]{1,2,0:T(8,128)} %fusion.231) | copy-start | bytes 3145732 | tf_op jit(solution)/shard_map/while
  117.0 3.2 copy-start.5
  159.1 1.0 copy-start.1
  164.5 4.8 copy-start.2
  164.5 7.5 %copy-start = (f32[4,256,256]{1,2,0:T(8,128)S(1)}, f32[4,256,256]{1,2,0:T(8,128)}, u32[]{:S(2)}) copy-start(f32[4,256,256]{1,2,0:T(8,128)} %fusion.231) | copy-start | bytes 3145732 | tf_op jit(solution)/shard_map/while
  177.3 3.9 copy-start.5
  221.0 1.0 copy-start.1
  226.4 4.6 copy-start.2
  226.4 7.2 %copy-start = (f32[4,256,256]{1,2,0:T(8,128)S(1)}, f32[4,256,256]{1,2,0:T(8,128)}, u32[]{:S(2)}) copy-start(f32[4,256,256]{1,2,0:T(8,128)} %fusion.231) | copy-start | bytes 3145732 | tf_op jit(solution)/shard_map/while
  239.0 3.9 copy-start.5
  282.7 1.0 copy-start.1
  288.0 4.6 copy-start.2
  288.1 7.3 %copy-start = (f32[4,256,256]{1,2,0:T(8,128)S(1)}, f32[4,256,256]{1,2,0:T(8,128)}, u32[]{:S(2)}) copy-start(f32[4,256,256]{1,2,0:T(8,128)} %fusion.231) | copy-start | bytes 3145732 | tf_op jit(solution)/shard_map/while
  300.7 3.9 copy-start.5
  522.3 5.7 copy-start.3
  526.2 165.7 %collective-permute-start.1 = (f32[512,2,512]{2,1,0:T(2,128)}, f32[512,2,512]{2,1,0:T(2,128)}, u32[]{:S(2)}, u32[]{:S(2)}) collective-permute-start(f32[512,2,512]{2,1,0:T(2,128)} %slice.43), channel_id=1, source_target_pairs={{0,8},{8,16},{16,24},{24,32},{32,40},{40,48},{48,56},{56,64},{64,7... | collective-permute-start | bytes 6291464 | tf_op jit(solution)/shard_map/ppermute | solution.py:13
  529.6 1.6 copy-start.6
  688.4 3.4 copy-start.4
  688.4 4.2 copy-start.8
Sparse Core Ops, SparseCore 0:
  529.8 157.6 all-reduce.2
where the time goes:
time: 710 us; the launch traced here: 705 us
  local copies, waits for them, and re-layouts  230 us (32%)
  matrix products  201 us (28%)
  waiting for transfers between devices  178 us (25%)
  other arithmetic  53.2 us (7%)
  loops' own time  23.3 us (3%)
  between operations  14.3 us (2%)
    dynamic_update_slice x4, local copies, waits for them, and re-layouts, put(): lax.dynamic_update_slice(scratch_array, current + wgrads[position_entry],...  180 us
    psum x1, waiting for transfers between devices, on_device(): pgrad, cover = lax.psum((pgrad, cover), ('region', 'group'))  155 us
    dot_general x8, matrix products, transform(): jnp.einsum('mjk,kl->mjl', left_i, sin_tab, precision=highest)  32.1 us
    dot_general x8, matrix products, transform(): jnp.einsum('mjk,kl->mjl', left_i, cos_tab, precision=highest)  29.2 us
    dot_general x8, matrix products, transform(): jnp.einsum('jk,mkl->mjl', sin_tab, real_part, precision=highest)  25.5 us
    dot_general x8, matrix products, transform(): jnp.einsum('mjk,kl->mjl', left_r, sin_tab, precision=highest)  25.3 us
    dot_general x8, matrix products, transform(): jnp.einsum('mjk,kl->mjl', left_r, cos_tab, precision=highest)  22.6 us
    ppermute x2, waiting for transfers between devices, shifted(): return lax.ppermute(block, axis, route)  22.5 us
  transfers between devices with their start and end apart: 3, of which 2 were waited for; matrix products, arithmetic and copies ran while one was open for 1% of the time, Pallas kernels for 0%

commit v1 on v0

--- a/solution.py
+++ b/solution.py
@@ -96,7 +96,7 @@
         jnp.zeros((side, side), jnp.float32),
     )
     wgrads, pgrad, cover = lax.fori_loop(0, slots, single_position, start_carry)
-    pgrad, cover = lax.psum((pgrad, cover), ("region", "group"))
+    pgrad, cover = lax.psum(lax.psum((pgrad, cover), "group"), "region")
 
     def put(position_entry, scratch_array):
         row = local_rows[position_entry]

time: 710 us -> 680 us (0.958)
  waiting for transfers between devices: 178 us -> 145 us
    psum x1 -> x2, waiting for transfers between devices: 155 us -> 97.2 us  [on_device(): pgrad, cover = lax.psum(lax.psum((pgrad, cover), 'group'), 'region')]
    ppermute x2, waiting for transfers between devices: 22.5 us -> 48.1 us  [shifted(): return lax.ppermute(block, axis, route)]
  transfers between devices with their start and end apart: 3 -> 4, of which waited for: 2 -> 3; matrix products, arithmetic and copies ran while one was open for 1% -> 31% of each run, Pallas kernels for 0% -> 0%
where the time goes in v1:
time: 680 us; the launch traced here: 674 us
  local copies, waits for them, and re-layouts  230 us (34%)
  matrix products  200 us (29%)
  waiting for transfers between devices  145 us (21%)
  other arithmetic  53.4 us (8%)
  loops' own time  25 us (4%)
  between operations  14.3 us (2%)
    dynamic_update_slice x4, local copies, waits for them, and re-layouts, put(): lax.dynamic_update_slice(scratch_array, current + wgrads[position_entry],...  180 us
    psum x2, waiting for transfers between devices, on_device(): pgrad, cover = lax.psum(lax.psum((pgrad, cover), 'group'), 'region')  97.2 us
    ppermute x2, waiting for transfers between devices, shifted(): return lax.ppermute(block, axis, route)  48.1 us
    dot_general x8, matrix products, transform(): jnp.einsum('mjk,kl->mjl', left_i, sin_tab, precision=highest)  32.1 us
    dot_general x8, matrix products, transform(): jnp.einsum('mjk,kl->mjl', left_i, cos_tab, precision=highest)  29.2 us
    dot_general x8, matrix products, transform(): jnp.einsum('jk,mkl->mjl', sin_tab, real_part, precision=highest)  25.5 us
    dot_general x8, matrix products, transform(): jnp.einsum('mjk,kl->mjl', left_r, sin_tab, precision=highest)  25.3 us
    dot_general x8, matrix products, transform(): jnp.einsum('mjk,kl->mjl', left_r, cos_tab, precision=highest)  22.6 us
  transfers between devices with their start and end apart: 4, of which 3 were waited for; matrix products, arithmetic and copies ran while one was open for 31% of the time, Pallas kernels for 0%

profile of v1, /device:TPU:1, one launch (start us, length us, event | category | flops | bytes accessed | tf_op | source)
XLA Modules:
  0.0 673.8 jit_solution(14196540047757797009)
XLA Ops:
  13.6 22.5 %collective-permute-done = f32[512,2,512]{2,1,0:T(2,128)} collective-permute-done((f32[512,2,512]{2,1,0:T(2,128)}, f32[512,2,512]{2,1,0:T(2,128)}, u32[]{:S(2)}, u32[]{:S(2)}) %collective-permute-start) | collective-permute-done | bytes 2097184 | tf_op jit(solution)/shard_map/ppermute | solution.py:13
  36.2 5.3 pad_maximum_fusion
  43.4 17.9 %while.35 = (s32[]{:T(128)}, f32[1024,2,512]{2,1,0:T(2,128)}, s32[4,3]{1,0:T(4,128)S(1)}, f32[4,256,2,256]{3,2,1,0:T(2,128)}, s32[]{:T(128)}) while((s32[]{:T(128)}, f32[1024,2,512]{2,1,0:T(2,128)}, s32[4,3]{1,0:T(4,128)S(1)}, f32[4,256,2,256]{3,2,1,0:T(2,128)}, s32[]{:T(128)}) %tuple.99), condition=%wide.while_cond, body=%wide.while_body.sunk | while | flops 2 | bytes 1050217 | solution.py:56
  44.0 3.8 bitcast_dynamic-update-slice_fusion.2
  48.5 3.8 bitcast_dynamic-update-slice_fusion.2
  53.0 3.8 bitcast_dynamic-update-slice_fusion.2
  57.4 3.8 bitcast_dynamic-update-slice_fusion.2
  63.1 249.8 %while.36 = (s32[]{:T(128)}, f32[4,256,2,256]{3,2,1,0:T(2,128)}, f32[4,2,256,256]{3,2,0,1:T(8,128)}, f32[256,256]{1,0:T(8,128)}, f32[4,256,2,256]{3,2,1,0:T(2,12...) while((s32[]{:T(128)}, f32[4,256,2,256]{3,2,1,0:T(2,128)}, ...), condition=%wide.region_4.5_spmd.clone.clone, body=%wide.region_0.4_spmd.clone.clone.sunk | while | flops 12915048448 | bytes 82838280 | solution.py:98
  90.8 3.6 fusion.231
  100.8 3.7 fusion.229
  105.1 4.6 fusion.232
  112.4 5.3 add_bitcast_fusion.2
  160.8 3.7 fusion.229
  165.2 4.8 fusion.232
  172.7 5.3 add_bitcast_fusion.2
  178.0 3.9 maximum_add_fusion.2
  222.7 3.7 fusion.229
  227.1 4.5 fusion.232
  234.3 5.3 add_bitcast_fusion.2
  239.6 3.9 maximum_add_fusion.2
  284.4 3.7 fusion.229
  288.7 4.6 fusion.232
  296.0 5.3 add_bitcast_fusion.2
  301.3 3.9 maximum_add_fusion.2
  319.1 209.1 %while.34 = (s32[]{:T(128)}, f32[1024,2,512]{2,1,0:T(2,128)}, s32[4]{0:T(128)S(1)}, s32[4]{0:T(128)S(1)}, f32[4,256,2,256]{3,2,1,0:T(2,128)}, /*index=5*/s32[]{:T(128)}, s32[]{:T(128)}, s32[]{:T(128)}, s32[]{:T(128)}) while((s32[]{:T(128)}, f32[1024,2,512]{2,1,0:T(2,128)}, s32[4]{0:T(128)S(1)}, s32[4]{0:T(128)S(1)}, ...), condition=%wide.region_6.7_spmd, body=%wide.region_5.6_spmd.sunk | while | flops 131080 | bytes 2621641 | solution.py:109
  326.4 45.0 %dynamic_update_slice.21 = f32[1024,2,512]{2,1,0:T(2,128)} dynamic-update-slice(f32[1024,2,512]{2,1,0:T(2,128)} %get-tuple-element.737, f32[256,2,256]{2,1,0:T(2,128)S(1)} %bitcast_add_fusion.2, s32[]{:T(128)S(6)} %select_n.175, s32[]{:T(128)} %constant.116.clone.1..sunk, s32[]{:T(128)S(6)} %select_n.176) | dynamic-update-slice | bytes 1048580 | tf_op jit(solution)/shard_map/while/body/eval_jaxpr/dynamic_update_slice | solution.py:105
  378.7 45.0 %dynamic_update_slice.21 = f32[1024,2,512]{2,1,0:T(2,128)} dynamic-update-slice(f32[1024,2,512]{2,1,0:T(2,128)} %get-tuple-element.737, f32[256,2,256]{2,1,0:T(2,128)S(1)} %bitcast_add_fusion.2, s32[]{:T(128)S(6)} %select_n.175, s32[]{:T(128)} %constant.116.clone.1..sunk, s32[]{:T(128)S(6)} %select_n.176) | dynamic-update-slice | bytes 1048580 | tf_op jit(solution)/shard_map/while/body/eval_jaxpr/dynamic_update_slice | solution.py:105
  430.9 45.0 %dynamic_update_slice.21 = f32[1024,2,512]{2,1,0:T(2,128)} dynamic-update-slice(f32[1024,2,512]{2,1,0:T(2,128)} %get-tuple-element.737, f32[256,2,256]{2,1,0:T(2,128)S(1)} %bitcast_add_fusion.2, s32[]{:T(128)S(6)} %select_n.175, s32[]{:T(128)} %constant.116.clone.1..sunk, s32[]{:T(128)S(6)} %select_n.176) | dynamic-update-slice | bytes 1048580 | tf_op jit(solution)/shard_map/while/body/eval_jaxpr/dynamic_update_slice | solution.py:105
  483.2 45.0 %dynamic_update_slice.21 = f32[1024,2,512]{2,1,0:T(2,128)} dynamic-update-slice(f32[1024,2,512]{2,1,0:T(2,128)} %get-tuple-element.737, f32[256,2,256]{2,1,0:T(2,128)S(1)} %bitcast_add_fusion.2, s32[]{:T(128)S(6)} %select_n.175, s32[]{:T(128)} %constant.116.clone.1..sunk, s32[]{:T(128)S(6)} %select_n.176) | dynamic-update-slice | bytes 1048580 | tf_op jit(solution)/shard_map/while/body/eval_jaxpr/dynamic_update_slice | solution.py:105
  534.7 25.6 %collective-permute-done.1 = f32[512,2,512]{2,1,0:T(2,128)} collective-permute-done((f32[512,2,512]{2,1,0:T(2,128)}, f32[512,2,512]{2,1,0:T(2,128)}, u32[]{:S(2)}, u32[]{:S(2)}) %collective-permute-start.1) | collective-permute-done | bytes 2097184 | tf_op jit(solution)/shard_map/ppermute | solution.py:13
  560.3 5.2 divide_subtract_fusion
  565.5 97.1 %all-reduce.5.cloned.1.call-done = (f32[4,2,256,256]{3,2,1,0:T(8,128)}, f32[256,256]{1,0:T(8,128)}) async-done(((f32[4,2,256,256]{3,2,1,0:T(8,128)}, f32[256,256]{1,0:T(8,128)}), (f32[4,2,256,256]{3,2,1,0:T(8,128)}, f32[256,256]{1,0:T(8,128)})) %all-reduce.5.cloned.1.call-update) | async-done | bytes 2359312 | tf_op jit(solution)/shard_map/psum | solution.py:99
  (166 shorter events, 213.9 us)
Async XLA Ops:
  7.2 526.7 %all-reduce.7.cloned.1.call-start = ((), (), s32[]{:S(2)}) async-start(), calls=%async_computation.1 | async-start | bytes 4718592 | tf_op jit(solution)/shard_map/psum | solution.py:99
  7.2 29.0 %collective-permute-start = (f32[512,2,512]{2,1,0:T(2,128)}, f32[512,2,512]{2,1,0:T(2,128)}, u32[]{:S(2)}, u32[]{:S(2)}) collective-permute-start(f32[512,2,512]{2,1,0:T(2,128)} %param.9), channel_id=1, source_target_pairs={{8,0},{16,8},{24,16},{32,24},{40,32},{48,40},{56,48},{64,56},{72,6... | collective-permute-start | bytes 6291464 | tf_op jit(solution)/shard_map/ppermute | solution.py:13
  11.7 24.5 %copy-start.5 = (f32[512,2,512]{2,1,0:T(2,128)S(1)}, f32[512,2,512]{2,1,0:T(2,128)}, u32[]{:S(2)}) copy-start(f32[512,2,512]{2,1,0:T(2,128)} %param.9) | copy-start | bytes 6291460
  99.8 1.0 copy-start.1
  105.1 4.6 copy-start.2
  105.1 7.3 %copy-start = (f32[4,256,256]{1,2,0:T(8,128)S(1)}, f32[4,256,256]{1,2,0:T(8,128)}, u32[]{:S(2)}) copy-start(f32[4,256,256]{1,2,0:T(8,128)} %fusion.231) | copy-start | bytes 3145732 | tf_op jit(solution)/shard_map/while
  117.8 3.2 copy-start.3
  159.8 1.0 copy-start.1
  165.2 4.8 copy-start.2
  165.2 7.5 %copy-start = (f32[4,256,256]{1,2,0:T(8,128)S(1)}, f32[4,256,256]{1,2,0:T(8,128)}, u32[]{:S(2)}) copy-start(f32[4,256,256]{1,2,0:T(8,128)} %fusion.231) | copy-start | bytes 3145732 | tf_op jit(solution)/shard_map/while
  178.0 3.9 copy-start.3
  221.7 1.0 copy-start.1
  227.0 4.6 copy-start.2
  227.1 7.2 %copy-start = (f32[4,256,256]{1,2,0:T(8,128)S(1)}, f32[4,256,256]{1,2,0:T(8,128)}, u32[]{:S(2)}) copy-start(f32[4,256,256]{1,2,0:T(8,128)} %fusion.231) | copy-start | bytes 3145732 | tf_op jit(solution)/shard_map/while
  239.6 3.9 copy-start.3
  283.4 1.0 copy-start.1
  288.7 4.6 copy-start.2
  288.7 7.3 %copy-start = (f32[4,256,256]{1,2,0:T(8,128)S(1)}, f32[4,256,256]{1,2,0:T(8,128)}, u32[]{:S(2)}) copy-start(f32[4,256,256]{1,2,0:T(8,128)} %fusion.231) | copy-start | bytes 3145732 | tf_op jit(solution)/shard_map/while
  301.3 3.9 copy-start.3
  316.0 346.6 %all-reduce.5.cloned.1.call-start = ((), (), s32[]{:S(2)}) async-start(), calls=%async_computation | async-start | bytes 4718592 | tf_op jit(solution)/shard_map/psum | solution.py:99
  531.8 2.1 copy-start.4
  531.8 28.5 %collective-permute-start.1 = (f32[512,2,512]{2,1,0:T(2,128)}, f32[512,2,512]{2,1,0:T(2,128)}, u32[]{:S(2)}, u32[]{:S(2)}) collective-permute-start(f32[512,2,512]{2,1,0:T(2,128)} %slice.43), channel_id=1, source_target_pairs={{0,8},{8,16},{16,24},{24,32},{32,40},{40,48},{48,56},{56,64},{64,7... | collective-permute-start | bytes 6291464 | tf_op jit(solution)/shard_map/ppermute | solution.py:13
Sparse Core Ops, SparseCore 0:
  316.1 94.2 all-reduce.6
  534.0 128.5 all-reduce.4
